TPU v7x, 512 devices: a whole 4x4x16 slice. The times are simulated.
512 devices in a mesh: pipe: 16 (over z_hi, y), dp: 32 (over x, z_lo, core).
Axes of the slice: x: 4, y: 4, z: 16 (z_hi: 4, z_lo: 4; z = z_hi * 4 + z_lo), core: 2. Of those that a mesh axis runs over, the one named last changes fastest.
Arguments:
- episode_states: bfloat16 [2, 2, 1024, 896], P(None, None, 'dp'), may hold values from -200 to 200
- norm_gain: bfloat16 [16, 896], P('pipe', 'dp'), may hold values from 0.099609375 to 1.8984375
- qkv_weight: bfloat16 [16, 896, 576], P('pipe', 'dp'), may hold values from -10 to 10
- out_weight: bfloat16 [16, 448, 896], P('pipe', 'dp'), may hold values from -0.25 to 0.25
- final_gain: bfloat16 [896], replicated, may hold values from 0.099609375 to 1.8984375
- value_weight: bfloat16 [896], replicated, may hold values from -0.1875 to 0.1875
- target_positions: int32 [2, 2, 32, 16], P(None, None, 'dp'), may hold values from 0 to 31
- value_targets: float32 [2, 2, 32, 16], P(None, None, 'dp'), may hold values from -4 to 4
Outputs:
- grad_gain: float32 [16, 896], P('pipe', 'dp')
- grad_qkv: float32 [16, 896, 576], P('pipe', 'dp')
- grad_out: float32 [16, 448, 896], P('pipe', 'dp')
Inputs may be any that keep to these rules, and one draw needn't show every extreme that they name: `target_positions`: positions inside one window of 32 tokens; a position may appear more than once.
All inputs are finite; a program needn't handle non-finite values.
Results may differ from a plain program's by a relative error of at most 0.035.
Values may be sent and summed in bfloat16 or wider, within the bound.
A program may use at most 64 MiB of HBM per device.

v0:
```python
import math

import jax
import jax.numpy as jnp
from jax import lax
from jax.sharding import PartitionSpec as P

HEAD = 64
QHEADS = 7


def partner_2(block, axis, bit):
    count = lax.axis_size(axis)
    route = []
    for low in range(count):
        high = low | 1 << bit
        if high != low and high < count:
            route += [(low, high), (high, low)]
    return lax.ppermute(block, axis, route)


def extended(cells, sides, width):
    for axis, dim in sides:
        count = lax.axis_size(axis)
        ends = count - 1
        head = lax.slice_in_dim(cells, 0, width, axis=dim)
        tail = lax.slice_in_dim(cells, cells.shape[dim] - width, cells.shape[dim], axis=dim)
        cells = jnp.concatenate(
            [
                lax.ppermute(tail, axis, [(i, (i + 1) % count) for i in range(ends)]),
                cells,
                lax.ppermute(head, axis, [((i + 1) % count, i) for i in range(ends)]),
            ],
            axis=dim,
        )
    return cells


def section_apply(states, norm_scale, qkv_mat, out_mat):
    row_count = states.shape[0]
    query_width = QHEADS * HEAD
    widened = states.astype(jnp.float32)
    inverse_rms = lax.rsqrt(jnp.mean(widened * widened, axis=-1, keepdims=True) + 1e-06)
    normed = (widened * inverse_rms * norm_scale.astype(jnp.float32)).astype(jnp.bfloat16)
    projected = jnp.dot(normed, qkv_mat, preferred_element_type=jnp.float32).astype(jnp.bfloat16)
    queries = projected[:, :query_width].reshape(row_count, QHEADS, HEAD)
    key_rows = projected[:, query_width : query_width + HEAD]
    value_rows = projected[:, query_width + HEAD :]
    scores = jnp.einsum("qhd,kd->hqk", queries, key_rows, preferred_element_type=jnp.float32) * (
        1.0 / math.sqrt(HEAD)
    )
    position = jnp.arange(row_count, dtype=jnp.int32)
    allowed = position[:, None] >= position[None, :]
    scores = jnp.where(allowed[None, :, :], scores, -1e30)
    row_max = jnp.max(scores, axis=-1, keepdims=True)
    weights = jnp.exp(scores - row_max)
    attention = (weights / jnp.sum(weights, axis=-1, keepdims=True)).astype(jnp.bfloat16)
    attended = jnp.einsum("hqk,kd->qhd", attention, value_rows, preferred_element_type=jnp.float32)
    attended = attended.astype(jnp.bfloat16).reshape(row_count, query_width)
    update = jnp.dot(attended, out_mat, preferred_element_type=jnp.float32)
    return (widened + update).astype(jnp.bfloat16)


def value_loss(final_states, final_scale, head_weight, chosen, wanted):
    widened = final_states.astype(jnp.float32)
    inverse_rms = lax.rsqrt(jnp.mean(widened * widened, axis=-1, keepdims=True) + 1e-06)
    predicted = jnp.sum(
        widened * inverse_rms * final_scale.astype(jnp.float32) * head_weight.astype(jnp.float32),
        axis=-1,
    )
    selector = (
        chosen[:, None] == jnp.arange(final_states.shape[0], dtype=jnp.int32)[None, :]
    ).astype(jnp.float32)
    picked = jnp.sum(selector * predicted[None, :], axis=-1)
    residual = picked - wanted
    return 0.5 * jnp.sum(residual * residual)


def section_pullback(states, cotangent, norm_scale, qkv_mat, out_mat):
    unused, pullback = jax.vjp(section_apply, states, norm_scale, qkv_mat, out_mat)
    return pullback(cotangent)


def mirror_weights(gain_piece, qkv_piece, out_piece):
    pipe_count = lax.axis_size("pipe")
    result = (gain_piece, qkv_piece, out_piece)
    for bit_number in range(pipe_count.bit_length() - 1):
        result = partner_2((result[0], result[1], result[2]), "pipe", bit_number)
    return result


def mirror_shards(gain_piece, qkv_piece, out_piece):
    pipe_count = lax.axis_size("pipe")
    result = (gain_piece, qkv_piece, out_piece)
    for bit_number in range(pipe_count.bit_length() - 1):
        result = (
            partner_2(result[0].astype(jnp.bfloat16), "pipe", bit_number).astype(jnp.float32),
            partner_2(result[1].astype(jnp.bfloat16), "pipe", bit_number).astype(jnp.float32),
            partner_2(result[2].astype(jnp.bfloat16), "pipe", bit_number).astype(jnp.float32),
        )
    return result


def per_device(
    episode_states,
    norm_gain,
    qkv_weight,
    out_weight,
    final_gain,
    value_weight,
    target_positions,
    value_targets,
):
    pipe_count = lax.axis_size("pipe")
    pipe_index = lax.axis_index("pipe")
    last_index = pipe_count - 1
    micro_count = episode_states.shape[1]
    row_count = episode_states.shape[2]
    model_width = episode_states.shape[3]
    mirrored = mirror_weights(norm_gain[0], qkv_weight[0], out_weight[0])
    gain_rows, qkv_rows, out_rows = (
        lax.all_gather(jnp.stack([norm_gain[0], mirrored[0]]), "dp", axis=1, tiled=True),
        lax.all_gather(jnp.stack([qkv_weight[0], mirrored[1]]), "dp", axis=1, tiled=True),
        lax.all_gather(jnp.stack([out_weight[0], mirrored[2]]), "dp", axis=1, tiled=True),
    )
    backward_start = pipe_count + micro_count - 1
    tick_count = backward_start + pipe_count + micro_count - 1
    positions = target_positions[:, :, 0]
    goal_values = value_targets[:, :, 0]
    blank_rows = jnp.zeros((row_count, model_width), jnp.bfloat16)

    def blank_like(operand):
        return jnp.zeros_like(operand)

    def slot_of(step_index, start):
        slot_offset = step_index - start
        active = (slot_offset >= 0) & (slot_offset < micro_count)
        slot_index = jnp.clip(slot_offset, 0, micro_count - 1)
        return (active, slot_index)

    def forward_pass(
        copy_index,
        start,
        incoming,
        entry_device,
        exit_device,
        step_index,
        stored_inputs,
        exit_cotangents,
    ):
        active, slot_index = slot_of(step_index, start)
        entering = lax.dynamic_index_in_dim(
            episode_states[copy_index], slot_index, 0, keepdims=False
        )
        inputs = jnp.where(pipe_index == entry_device, entering, incoming)
        previous = lax.dynamic_index_in_dim(
            stored_inputs[copy_index], slot_index, 0, keepdims=False
        )
        kept = jnp.where(active, inputs, previous)
        corner = (jnp.int32(copy_index), slot_index, jnp.int32(0), jnp.int32(0))
        stored_inputs = lax.dynamic_update_slice(stored_inputs, kept[None, None], corner)

        def forward_compute(operand):
            return section_apply(
                operand, gain_rows[copy_index], qkv_rows[copy_index], out_rows[copy_index]
            )

        produced = lax.cond(active, forward_compute, blank_like, inputs)
        at_exit = active & (pipe_index == exit_device)

        def start_backward(operand):
            chosen = lax.dynamic_index_in_dim(positions[copy_index], slot_index, 0, keepdims=False)
            wanted = lax.dynamic_index_in_dim(
                goal_values[copy_index], slot_index, 0, keepdims=False
            )
            return jax.grad(value_loss)(operand, final_gain, value_weight, chosen, wanted)

        cotangent = lax.cond(at_exit, start_backward, blank_like, produced)
        previous_cot = lax.dynamic_index_in_dim(
            exit_cotangents[copy_index], slot_index, 0, keepdims=False
        )
        exit_cotangents = lax.dynamic_update_slice(
            exit_cotangents, jnp.where(at_exit, cotangent, previous_cot)[None, None], corner
        )
        outbound = jnp.where(pipe_index == exit_device, blank_rows, produced)
        return (outbound, stored_inputs, exit_cotangents)

    def backward_pass(
        copy_index,
        start,
        incoming,
        exit_device,
        step_index,
        stored_inputs,
        exit_cotangents,
        gradients,
    ):
        active, slot_index = slot_of(step_index, start)
        states = lax.dynamic_index_in_dim(stored_inputs[copy_index], slot_index, 0, keepdims=False)
        own_cot = lax.dynamic_index_in_dim(
            exit_cotangents[copy_index], slot_index, 0, keepdims=False
        )
        arriving = jnp.where(pipe_index == exit_device, own_cot, incoming)

        def backward_compute(operands):
            pulled = section_pullback(
                operands[0],
                operands[1],
                gain_rows[copy_index],
                qkv_rows[copy_index],
                out_rows[copy_index],
            )
            updated = tuple(
                (
                    running.at[copy_index].add(increment.astype(jnp.float32))
                    for running, increment in zip(operands[2:], pulled[1:])
                )
            )
            return (pulled[0],) + updated

        def pass_over(operands):
            return (jnp.zeros_like(operands[0]),) + tuple(operands[2:])

        results = lax.cond(
            active, backward_compute, pass_over, (states, arriving) + tuple(gradients)
        )
        return (results[0], tuple(results[1:]))

    def advance(step_index, state_tuple):
        from_prev, from_next, stored_inputs, exit_cotangents, gradients = state_tuple
        ahead_first, stored_inputs, exit_cotangents = forward_pass(
            0, pipe_index, from_prev, 0, last_index, step_index, stored_inputs, exit_cotangents
        )
        ahead_second, stored_inputs, exit_cotangents = forward_pass(
            1,
            last_index - pipe_index,
            from_next,
            last_index,
            0,
            step_index,
            stored_inputs,
            exit_cotangents,
        )
        back_first, gradients = backward_pass(
            0,
            backward_start + last_index - pipe_index,
            from_next,
            last_index,
            step_index,
            stored_inputs,
            exit_cotangents,
            gradients,
        )
        back_second, gradients = backward_pass(
            1,
            backward_start + pipe_index,
            from_prev,
            0,
            step_index,
            stored_inputs,
            exit_cotangents,
            gradients,
        )
        outgoing = jnp.stack([ahead_second + back_first, ahead_first + back_second])
        padded = extended(outgoing, (("pipe", 0),), 1)
        return (padded[0], padded[3], stored_inputs, exit_cotangents, gradients)

    stored_init = jnp.zeros((2, micro_count, row_count, model_width), jnp.bfloat16)
    gradients_init = (
        jnp.zeros(gain_rows.shape, jnp.float32),
        jnp.zeros(qkv_rows.shape, jnp.float32),
        jnp.zeros(out_rows.shape, jnp.float32),
    )
    final_tuple = lax.fori_loop(
        0, tick_count, advance, (blank_rows, blank_rows, stored_init, stored_init, gradients_init)
    )
    gradients = final_tuple[4]
    rounded = tuple(
        (
            lax.optimization_barrier(running.astype(jnp.bfloat16)).astype(jnp.float32)
            for running in gradients
        )
    )
    summed = (
        lax.psum_scatter(
            rounded[0].astype(jnp.bfloat16), "dp", scatter_dimension=1, tiled=True
        ).astype(jnp.float32),
        lax.psum_scatter(
            rounded[1].astype(jnp.bfloat16), "dp", scatter_dimension=1, tiled=True
        ).astype(jnp.float32),
        lax.psum_scatter(
            rounded[2].astype(jnp.bfloat16), "dp", scatter_dimension=1, tiled=True
        ).astype(jnp.float32),
    )
    partner = mirror_shards(summed[0][1], summed[1][1], summed[2][1])
    grad_gain = (summed[0][0] + partner[0])[None]
    grad_qkv = (summed[1][0] + partner[1])[None]
    grad_out = (summed[2][0] + partner[2])[None]
    return (grad_gain, grad_qkv, grad_out)


def solution(mesh):
    return jax.shard_map(
        per_device,
        mesh=mesh,
        in_specs=(
            P(None, None, "dp", None),
            P("pipe", "dp"),
            P("pipe", "dp", None),
            P("pipe", "dp", None),
            P(),
            P(),
            P(None, None, "dp", None),
            P(None, None, "dp", None),
        ),
        out_specs=(P("pipe", "dp"), P("pipe", "dp", None), P("pipe", "dp", None)),
        check_vma=False,
    )
```

profile of v0, /device:TPU:1, one launch (start us, length us, event | category | flops | bytes accessed | tf_op | source)
XLA Modules:
  0.0 2129.6 jit_solution(12559435727906046938)
XLA Ops:
  29.0 13.9 collective-permute-start.13
  66.7 10.9 collective-permute-start.9
  101.4 10.3 collective-permute-start.5
  115.1 54.4 %all-gather = bf16[32,28,2]{1,2,0:T(2,128)(2,1)S(1)} all-gather(bf16[1,28,2]{1,2,0:T(2,128)(2,1)S(1)} %maximum_bitcast_fusion), channel_id=1, replica_groups=mesh['pipe'=16,'dp'=32] {'dp'}, dimensions={0}, use_global_device_ids=true | all-gather | bytes 3696 | tf_op jit(solution)/shard_map/all_gather | solution.py:122
  172.9 12.0 all-gather.4.cloned.1.call-done
  192.7 1515.2 %while.32 = (s32[]{:T(128)}, bf16[32,896]{1,0:T(8,128)(2,1)S(1)}, bf16[32,896]{1,0:T(8,128)(2,1)S(1)}, bf16[2,2,32,896]{3,2,1,0:T(8,128)(2,1)}, bf16[2,2,32,896]...) while((s32[]{:T(128)}, bf16[32,896]{1,0:T(8,128)(2,1)S(1)}, ...), condition=%wide.region_45.46_spmd, body=%wide.region_0.45_spmd.sunk | while | flops 445446240 | bytes 54549096 | solution.py:274
  349.0 14.1 collective-permute-start
  501.5 10.4 collective-permute-start
  532.1 22.5 %collective-permute-start = (bf16[1,32,896]{2,1,0:T(8,128)(2,1)S(1)}, bf16[1,32,896]{2,1,0:T(8,128)(2,1)S(1)}, u32[]{:S(2)}, u32[]{:S(2)}) collective-permute-start(bf16[1,32,896]{2,1,0:T(8,128)(2,1)S(1)} %add_bitcast_fusion.4), channel_id=1, source_target_pairs={{0,32},{32,64},{64,96},{96,128},{128,160},{160,192},{192,224},{224... | collective-permute-start | bytes 172040 | tf_op jit(solution)/shard_map/while/body/eval_jaxpr/ppermute | solution.py:30
  581.1 14.4 collective-permute-start
  597.7 10.1 collective-permute-done.1
  622.1 16.0 collective-permute-start
  664.7 14.4 collective-permute-start
  762.3 31.2 %conditional.17 = (bf16[32,896]{1,0:T(8,128)(2,1)}, f32[2,896]{1,0:T(2,128)}, f32[2,896,576]{1,2,0:T(8,128)}, f32[2,448,896]{2,1,0:T(8,128)S(1)}) conditional(s32[]{:T(128)} %convert_element_type.728, (f32[2,896]{1,0:T(2,128)}, f32[2,896,576]{1,2,0:T(8,128)}, f32[2,448,896]{2,1,0:T(8,128)S(1)}) %tuple.167, (bf16[2,2,32,896]{3,2,1,0:T(8,128)(2,1)}, ...), branch_computations={%region_35.35_spmd, %region_36.44_spmd} | conditional | flops 160113600 | bytes 22189488 | solution.py:224
  814.2 31.2 %conditional.17 = (bf16[32,896]{1,0:T(8,128)(2,1)}, f32[2,896]{1,0:T(2,128)}, f32[2,896,576]{1,2,0:T(8,128)}, f32[2,448,896]{2,1,0:T(8,128)S(1)}) conditional(s32[]{:T(128)} %convert_element_type.728, (f32[2,896]{1,0:T(2,128)}, f32[2,896,576]{1,2,0:T(8,128)}, f32[2,448,896]{2,1,0:T(8,128)S(1)}) %tuple.167, (bf16[2,2,32,896]{3,2,1,0:T(8,128)(2,1)}, ...), branch_computations={%region_35.35_spmd, %region_36.44_spmd} | conditional | flops 160113600 | bytes 22189488 | solution.py:224
  868.0 32.5 %collective-permute-start = (bf16[1,32,896]{2,1,0:T(8,128)(2,1)S(1)}, bf16[1,32,896]{2,1,0:T(8,128)(2,1)S(1)}, u32[]{:S(2)}, u32[]{:S(2)}) collective-permute-start(bf16[1,32,896]{2,1,0:T(8,128)(2,1)S(1)} %add_bitcast_fusion.4), channel_id=1, source_target_pairs={{0,32},{32,64},{64,96},{96,128},{128,160},{160,192},{192,224},{224... | collective-permute-start | bytes 172040 | tf_op jit(solution)/shard_map/while/body/eval_jaxpr/ppermute | solution.py:30
  924.6 32.4 %collective-permute-done.1 = bf16[1,32,896]{2,1,0:T(8,128)(2,1)S(1)} collective-permute-done((bf16[1,32,896]{2,1,0:T(8,128)(2,1)S(1)}, bf16[1,32,896]{2,1,0:T(8,128)(2,1)S(1)}, u32[]{:S(2)}, u32[]{:S(2)}) %collective-permute-start.1) | collective-permute-done | bytes 57376 | tf_op jit(solution)/shard_map/while/body/eval_jaxpr/ppermute | solution.py:32
  994.9 36.8 %collective-permute-start = (bf16[1,32,896]{2,1,0:T(8,128)(2,1)S(1)}, bf16[1,32,896]{2,1,0:T(8,128)(2,1)S(1)}, u32[]{:S(2)}, u32[]{:S(2)}) collective-permute-start(bf16[1,32,896]{2,1,0:T(8,128)(2,1)S(1)} %add_bitcast_fusion.4), channel_id=1, source_target_pairs={{0,32},{32,64},{64,96},{96,128},{128,160},{160,192},{192,224},{224... | collective-permute-start | bytes 172040 | tf_op jit(solution)/shard_map/while/body/eval_jaxpr/ppermute | solution.py:30
  1061.9 32.4 %collective-permute-done.1 = bf16[1,32,896]{2,1,0:T(8,128)(2,1)S(1)} collective-permute-done((bf16[1,32,896]{2,1,0:T(8,128)(2,1)S(1)}, bf16[1,32,896]{2,1,0:T(8,128)(2,1)S(1)}, u32[]{:S(2)}, u32[]{:S(2)}) %collective-permute-start.1) | collective-permute-done | bytes 57376 | tf_op jit(solution)/shard_map/while/body/eval_jaxpr/ppermute | solution.py:32
  1138.1 24.7 %collective-permute-start = (bf16[1,32,896]{2,1,0:T(8,128)(2,1)S(1)}, bf16[1,32,896]{2,1,0:T(8,128)(2,1)S(1)}, u32[]{:S(2)}, u32[]{:S(2)}) collective-permute-start(bf16[1,32,896]{2,1,0:T(8,128)(2,1)S(1)} %add_bitcast_fusion.4), channel_id=1, source_target_pairs={{0,32},{32,64},{64,96},{96,128},{128,160},{160,192},{192,224},{224... | collective-permute-start | bytes 172040 | tf_op jit(solution)/shard_map/while/body/eval_jaxpr/ppermute | solution.py:30
  1195.0 24.7 %collective-permute-done.1 = bf16[1,32,896]{2,1,0:T(8,128)(2,1)S(1)} collective-permute-done((bf16[1,32,896]{2,1,0:T(8,128)(2,1)S(1)}, bf16[1,32,896]{2,1,0:T(8,128)(2,1)S(1)}, u32[]{:S(2)}, u32[]{:S(2)}) %collective-permute-start.1) | collective-permute-done | bytes 57376 | tf_op jit(solution)/shard_map/while/body/eval_jaxpr/ppermute | solution.py:32
  1264.1 57.4 %collective-permute-start = (bf16[1,32,896]{2,1,0:T(8,128)(2,1)S(1)}, bf16[1,32,896]{2,1,0:T(8,128)(2,1)S(1)}, u32[]{:S(2)}, u32[]{:S(2)}) collective-permute-start(bf16[1,32,896]{2,1,0:T(8,128)(2,1)S(1)} %add_bitcast_fusion.4), channel_id=1, source_target_pairs={{0,32},{32,64},{64,96},{96,128},{128,160},{160,192},{192,224},{224... | collective-permute-start | bytes 172040 | tf_op jit(solution)/shard_map/while/body/eval_jaxpr/ppermute | solution.py:30
  1323.7 34.8 %collective-permute-done.1 = bf16[1,32,896]{2,1,0:T(8,128)(2,1)S(1)} collective-permute-done((bf16[1,32,896]{2,1,0:T(8,128)(2,1)S(1)}, bf16[1,32,896]{2,1,0:T(8,128)(2,1)S(1)}, u32[]{:S(2)}, u32[]{:S(2)}) %collective-permute-start.1) | collective-permute-done | bytes 57376 | tf_op jit(solution)/shard_map/while/body/eval_jaxpr/ppermute | solution.py:32
  1372.8 39.1 %collective-permute-start = (bf16[1,32,896]{2,1,0:T(8,128)(2,1)S(1)}, bf16[1,32,896]{2,1,0:T(8,128)(2,1)S(1)}, u32[]{:S(2)}, u32[]{:S(2)}) collective-permute-start(bf16[1,32,896]{2,1,0:T(8,128)(2,1)S(1)} %add_bitcast_fusion.4), channel_id=1, source_target_pairs={{0,32},{32,64},{64,96},{96,128},{128,160},{160,192},{192,224},{224... | collective-permute-start | bytes 172040 | tf_op jit(solution)/shard_map/while/body/eval_jaxpr/ppermute | solution.py:30
  1414.1 34.8 %collective-permute-done.1 = bf16[1,32,896]{2,1,0:T(8,128)(2,1)S(1)} collective-permute-done((bf16[1,32,896]{2,1,0:T(8,128)(2,1)S(1)}, bf16[1,32,896]{2,1,0:T(8,128)(2,1)S(1)}, u32[]{:S(2)}, u32[]{:S(2)}) %collective-permute-start.1) | collective-permute-done | bytes 57376 | tf_op jit(solution)/shard_map/while/body/eval_jaxpr/ppermute | solution.py:32
  1463.2 40.9 %collective-permute-start = (bf16[1,32,896]{2,1,0:T(8,128)(2,1)S(1)}, bf16[1,32,896]{2,1,0:T(8,128)(2,1)S(1)}, u32[]{:S(2)}, u32[]{:S(2)}) collective-permute-start(bf16[1,32,896]{2,1,0:T(8,128)(2,1)S(1)} %add_bitcast_fusion.4), channel_id=1, source_target_pairs={{0,32},{32,64},{64,96},{96,128},{128,160},{160,192},{192,224},{224... | collective-permute-start | bytes 172040 | tf_op jit(solution)/shard_map/while/body/eval_jaxpr/ppermute | solution.py:30
  1506.3 34.8 %collective-permute-done.1 = bf16[1,32,896]{2,1,0:T(8,128)(2,1)S(1)} collective-permute-done((bf16[1,32,896]{2,1,0:T(8,128)(2,1)S(1)}, bf16[1,32,896]{2,1,0:T(8,128)(2,1)S(1)}, u32[]{:S(2)}, u32[]{:S(2)}) %collective-permute-start.1) | collective-permute-done | bytes 57376 | tf_op jit(solution)/shard_map/while/body/eval_jaxpr/ppermute | solution.py:32
  1555.4 39.4 %collective-permute-start = (bf16[1,32,896]{2,1,0:T(8,128)(2,1)S(1)}, bf16[1,32,896]{2,1,0:T(8,128)(2,1)S(1)}, u32[]{:S(2)}, u32[]{:S(2)}) collective-permute-start(bf16[1,32,896]{2,1,0:T(8,128)(2,1)S(1)} %add_bitcast_fusion.4), channel_id=1, source_target_pairs={{0,32},{32,64},{64,96},{96,128},{128,160},{160,192},{192,224},{224... | collective-permute-start | bytes 172040 | tf_op jit(solution)/shard_map/while/body/eval_jaxpr/ppermute | solution.py:30
  1612.3 31.8 %conditional.16 = (bf16[32,896]{1,0:T(8,128)(2,1)}, f32[2,896]{1,0:T(2,128)}, f32[2,896,576]{1,2,0:T(8,128)}, f32[2,448,896]{2,1,0:T(8,128)S(1)}) conditional(s32[]{:T(128)} %convert_element_type.729, (f32[2,896]{1,0:T(2,128)}, f32[2,896,576]{1,2,0:T(8,128)}, f32[2,448,896]{2,1,0:T(8,128)S(1)}) %tuple.157, (bf16[2,2,32,896]{3,2,1,0:T(8,128)(2,1)}, ...), branch_computations={%region_25.25_spmd, %region_26.34_spmd} | conditional | flops 160113600 | bytes 22418892 | solution.py:224
  1666.9 31.8 %conditional.16 = (bf16[32,896]{1,0:T(8,128)(2,1)}, f32[2,896]{1,0:T(2,128)}, f32[2,896,576]{1,2,0:T(8,128)}, f32[2,448,896]{2,1,0:T(8,128)S(1)}) conditional(s32[]{:T(128)} %convert_element_type.729, (f32[2,896]{1,0:T(2,128)}, f32[2,896,576]{1,2,0:T(8,128)}, f32[2,448,896]{2,1,0:T(8,128)S(1)}) %tuple.157, (bf16[2,2,32,896]{3,2,1,0:T(8,128)(2,1)}, ...), branch_computations={%region_25.25_spmd, %region_26.34_spmd} | conditional | flops 160113600 | bytes 22418892 | solution.py:224
  1725.2 107.6 %all-reduce.6 = bf16[2,896]{1,0:T(2,128)(2,1)S(1)} all-reduce(bf16[2,896]{1,0:T(2,128)(2,1)S(1)} %convert_element_type.485), channel_id=2, replica_groups=mesh['pipe'=16,'dp'=32] {'dp'}, use_global_device_ids=true, to_apply=%region_46.47.clone | all-reduce | flops 1792 | bytes 7168
  1832.9 219.4 %all-reduce.12.cloned.1.call-done = (bf16[2,896,576]{2,0,1:T(2,128)(2,1)}, bf16[2,448,896]{2,0,1:T(2,128)(2,1)}) async-done(((bf16[2,896,576]{2,0,1:T(2,128)(2,1)}, bf16[2,448,896]{2,0,1:T(2,128)(2,1)}), (bf16[2,896,576]{2,0,1:T(2,128)(2,1)}, bf16[2,448,896]{2,0,1:T(2,128)(2,1)})) %all-reduce.12.cloned.1.call-update) | async-done | bytes 3670032
  (1452 shorter events, 1190.7 us)
Async XLA Ops:
  7.2 163.0 %all-gather.6.cloned.1.call-start = ((), (), s32[]{:S(2)}) async-start(), calls=%async_computation.1 | async-start | bytes 1655808 | tf_op jit(solution)/shard_map/all_gather | solution.py:124
  29.0 15.1 collective-permute-start.13
  45.6 139.3 %all-gather.4.cloned.1.call-start = ((), (), s32[]{:S(2)}) async-start(), calls=%async_computation | async-start | bytes 2365440 | tf_op jit(solution)/shard_map/all_gather | solution.py:123
  66.7 14.4 collective-permute-start.9
  82.6 1969.6 %all-reduce.12.cloned.1.call-start = ((), (), s32[]{:S(2)}) async-start(), calls=%async_computation.2 | async-start | bytes 7798784
  101.4 13.0 collective-permute-start.5
  263.0 11.7 collective-permute-start
  349.0 16.2 collective-permute-start
  501.5 12.6 collective-permute-start
  532.1 24.6 %collective-permute-start = (bf16[1,32,896]{2,1,0:T(8,128)(2,1)S(1)}, bf16[1,32,896]{2,1,0:T(8,128)(2,1)S(1)}, u32[]{:S(2)}, u32[]{:S(2)}) collective-permute-start(bf16[1,32,896]{2,1,0:T(8,128)(2,1)S(1)} %add_bitcast_fusion.4), channel_id=1, source_target_pairs={{0,32},{32,64},{64,96},{96,128},{128,160},{160,192},{192,224},{224... | collective-permute-start | bytes 172040 | tf_op jit(solution)/shard_map/while/body/eval_jaxpr/ppermute | solution.py:30
  581.1 16.6 collective-permute-start
  622.1 18.2 collective-permute-start
  664.7 16.6 collective-permute-start
  868.0 34.6 %collective-permute-start = (bf16[1,32,896]{2,1,0:T(8,128)(2,1)S(1)}, bf16[1,32,896]{2,1,0:T(8,128)(2,1)S(1)}, u32[]{:S(2)}, u32[]{:S(2)}) collective-permute-start(bf16[1,32,896]{2,1,0:T(8,128)(2,1)S(1)} %add_bitcast_fusion.4), channel_id=1, source_target_pairs={{0,32},{32,64},{64,96},{96,128},{128,160},{160,192},{192,224},{224... | collective-permute-start | bytes 172040 | tf_op jit(solution)/shard_map/while/body/eval_jaxpr/ppermute | solution.py:30
  923.3 33.7 %collective-permute-start.1 = (bf16[1,32,896]{2,1,0:T(8,128)(2,1)S(1)}, bf16[1,32,896]{2,1,0:T(8,128)(2,1)S(1)}, u32[]{:S(2)}, u32[]{:S(2)}) collective-permute-start(bf16[1,32,896]{2,1,0:T(8,128)(2,1)S(1)} %add_bitcast_fusion.5), channel_id=1, source_target_pairs={{32,0},{64,32},{96,64},{128,96},{160,128},{192,160},{224,192},{256... | collective-permute-start | bytes 172040 | tf_op jit(solution)/shard_map/while/body/eval_jaxpr/ppermute | solution.py:32
  994.9 38.9 %collective-permute-start = (bf16[1,32,896]{2,1,0:T(8,128)(2,1)S(1)}, bf16[1,32,896]{2,1,0:T(8,128)(2,1)S(1)}, u32[]{:S(2)}, u32[]{:S(2)}) collective-permute-start(bf16[1,32,896]{2,1,0:T(8,128)(2,1)S(1)} %add_bitcast_fusion.4), channel_id=1, source_target_pairs={{0,32},{32,64},{64,96},{96,128},{128,160},{160,192},{192,224},{224... | collective-permute-start | bytes 172040 | tf_op jit(solution)/shard_map/while/body/eval_jaxpr/ppermute | solution.py:30
  1060.6 33.7 %collective-permute-start.1 = (bf16[1,32,896]{2,1,0:T(8,128)(2,1)S(1)}, bf16[1,32,896]{2,1,0:T(8,128)(2,1)S(1)}, u32[]{:S(2)}, u32[]{:S(2)}) collective-permute-start(bf16[1,32,896]{2,1,0:T(8,128)(2,1)S(1)} %add_bitcast_fusion.5), channel_id=1, source_target_pairs={{32,0},{64,32},{96,64},{128,96},{160,128},{192,160},{224,192},{256... | collective-permute-start | bytes 172040 | tf_op jit(solution)/shard_map/while/body/eval_jaxpr/ppermute | solution.py:32
  1138.1 26.8 %collective-permute-start = (bf16[1,32,896]{2,1,0:T(8,128)(2,1)S(1)}, bf16[1,32,896]{2,1,0:T(8,128)(2,1)S(1)}, u32[]{:S(2)}, u32[]{:S(2)}) collective-permute-start(bf16[1,32,896]{2,1,0:T(8,128)(2,1)S(1)} %add_bitcast_fusion.4), channel_id=1, source_target_pairs={{0,32},{32,64},{64,96},{96,128},{128,160},{160,192},{192,224},{224... | collective-permute-start | bytes 172040 | tf_op jit(solution)/shard_map/while/body/eval_jaxpr/ppermute | solution.py:30
  1183.0 12.0 collective-permute-start
  1193.7 26.1 %collective-permute-start.1 = (bf16[1,32,896]{2,1,0:T(8,128)(2,1)S(1)}, bf16[1,32,896]{2,1,0:T(8,128)(2,1)S(1)}, u32[]{:S(2)}, u32[]{:S(2)}) collective-permute-start(bf16[1,32,896]{2,1,0:T(8,128)(2,1)S(1)} %add_bitcast_fusion.5), channel_id=1, source_target_pairs={{32,0},{64,32},{96,64},{128,96},{160,128},{192,160},{224,192},{256... | collective-permute-start | bytes 172040 | tf_op jit(solution)/shard_map/while/body/eval_jaxpr/ppermute | solution.py:32
  1264.1 59.6 %collective-permute-start = (bf16[1,32,896]{2,1,0:T(8,128)(2,1)S(1)}, bf16[1,32,896]{2,1,0:T(8,128)(2,1)S(1)}, u32[]{:S(2)}, u32[]{:S(2)}) collective-permute-start(bf16[1,32,896]{2,1,0:T(8,128)(2,1)S(1)} %add_bitcast_fusion.4), channel_id=1, source_target_pairs={{0,32},{32,64},{64,96},{96,128},{128,160},{160,192},{192,224},{224... | collective-permute-start | bytes 172040 | tf_op jit(solution)/shard_map/while/body/eval_jaxpr/ppermute | solution.py:30
  1322.4 36.1 %collective-permute-start.1 = (bf16[1,32,896]{2,1,0:T(8,128)(2,1)S(1)}, bf16[1,32,896]{2,1,0:T(8,128)(2,1)S(1)}, u32[]{:S(2)}, u32[]{:S(2)}) collective-permute-start(bf16[1,32,896]{2,1,0:T(8,128)(2,1)S(1)} %add_bitcast_fusion.5), channel_id=1, source_target_pairs={{32,0},{64,32},{96,64},{128,96},{160,128},{192,160},{224,192},{256... | collective-permute-start | bytes 172040 | tf_op jit(solution)/shard_map/while/body/eval_jaxpr/ppermute | solution.py:32
  1372.8 41.3 %collective-permute-start = (bf16[1,32,896]{2,1,0:T(8,128)(2,1)S(1)}, bf16[1,32,896]{2,1,0:T(8,128)(2,1)S(1)}, u32[]{:S(2)}, u32[]{:S(2)}) collective-permute-start(bf16[1,32,896]{2,1,0:T(8,128)(2,1)S(1)} %add_bitcast_fusion.4), channel_id=1, source_target_pairs={{0,32},{32,64},{64,96},{96,128},{128,160},{160,192},{192,224},{224... | collective-permute-start | bytes 172040 | tf_op jit(solution)/shard_map/while/body/eval_jaxpr/ppermute | solution.py:30
  1412.8 36.1 %collective-permute-start.1 = (bf16[1,32,896]{2,1,0:T(8,128)(2,1)S(1)}, bf16[1,32,896]{2,1,0:T(8,128)(2,1)S(1)}, u32[]{:S(2)}, u32[]{:S(2)}) collective-permute-start(bf16[1,32,896]{2,1,0:T(8,128)(2,1)S(1)} %add_bitcast_fusion.5), channel_id=1, source_target_pairs={{32,0},{64,32},{96,64},{128,96},{160,128},{192,160},{224,192},{256... | collective-permute-start | bytes 172040 | tf_op jit(solution)/shard_map/while/body/eval_jaxpr/ppermute | solution.py:32
  1463.2 43.0 %collective-permute-start = (bf16[1,32,896]{2,1,0:T(8,128)(2,1)S(1)}, bf16[1,32,896]{2,1,0:T(8,128)(2,1)S(1)}, u32[]{:S(2)}, u32[]{:S(2)}) collective-permute-start(bf16[1,32,896]{2,1,0:T(8,128)(2,1)S(1)} %add_bitcast_fusion.4), channel_id=1, source_target_pairs={{0,32},{32,64},{64,96},{96,128},{128,160},{160,192},{192,224},{224... | collective-permute-start | bytes 172040 | tf_op jit(solution)/shard_map/while/body/eval_jaxpr/ppermute | solution.py:30
  1504.9 36.1 %collective-permute-start.1 = (bf16[1,32,896]{2,1,0:T(8,128)(2,1)S(1)}, bf16[1,32,896]{2,1,0:T(8,128)(2,1)S(1)}, u32[]{:S(2)}, u32[]{:S(2)}) collective-permute-start(bf16[1,32,896]{2,1,0:T(8,128)(2,1)S(1)} %add_bitcast_fusion.5), channel_id=1, source_target_pairs={{32,0},{64,32},{96,64},{128,96},{160,128},{192,160},{224,192},{256... | collective-permute-start | bytes 172040 | tf_op jit(solution)/shard_map/while/body/eval_jaxpr/ppermute | solution.py:32
  1555.4 41.6 %collective-permute-start = (bf16[1,32,896]{2,1,0:T(8,128)(2,1)S(1)}, bf16[1,32,896]{2,1,0:T(8,128)(2,1)S(1)}, u32[]{:S(2)}, u32[]{:S(2)}) collective-permute-start(bf16[1,32,896]{2,1,0:T(8,128)(2,1)S(1)} %add_bitcast_fusion.4), channel_id=1, source_target_pairs={{0,32},{32,64},{64,96},{96,128},{128,160},{160,192},{192,224},{224... | collective-permute-start | bytes 172040 | tf_op jit(solution)/shard_map/while/body/eval_jaxpr/ppermute | solution.py:30
  2063.6 34.3 %collective-permute-start.19 = (bf16[28,576]{1,0:T(8,128)(2,1)S(1)}, bf16[28,576]{1,0:T(8,128)(2,1)S(1)}, u32[]{:S(2)}, u32[]{:S(2)}) collective-permute-start(bf16[28,576]{1,0:T(8,128)(2,1)S(1)} %collective-permute-done.18), channel_id=1, source_target_pairs={{0,64},{64,0},{32,96},{96,32},{128,192},{192,128},{160,224},{224,1... | collective-permute-start | bytes 96776 | tf_op jit(solution)/shard_map/ppermute | solution.py:19
  2066.5 37.2 %collective-permute-start.24 = (bf16[14,896]{1,0:T(8,128)(2,1)S(1)}, bf16[14,896]{1,0:T(8,128)(2,1)S(1)}, u32[]{:S(2)}, u32[]{:S(2)}) collective-permute-start(bf16[14,896]{1,0:T(8,128)(2,1)S(1)} %collective-permute-done.23), channel_id=1, source_target_pairs={{0,128},{128,0},{32,160},{160,32},{64,192},{192,64},{96,224},{224,... | collective-permute-start | bytes 75272 | tf_op jit(solution)/shard_map/ppermute | solution.py:19
  2091.7 16.6 collective-permute-start.17
  2103.7 14.5 collective-permute-start.25
  2108.8 13.6 collective-permute-start.21
  (174 other events, 857.6 us)
Sparse Core Ops, SparseCore 0:
  45.7 71.6 all-gather.5
  120.1 64.7 all-gather.3
  1722.8 329.4 all-reduce.11
where the time goes:
time: 2150 us; the launch traced here: 2130 us
  starting transfers between devices  645 us (30%)
  waiting for transfers between devices  598 us (28%)
  local copies, waits for them, and re-layouts  399 us (19%)
  other arithmetic  217 us (10%)
  blocking collectives  162 us (8%)
  matrix products  88 us (4%)
    ppermute x34, starting transfers between devices, extended(): lax.ppermute(tail, axis, [(i, (i + 1) % count) for i in range(ends)])  471 us
    ppermute x34, waiting for transfers between devices, extended(): lax.ppermute(head, axis, [((i + 1) % count, i) for i in range(ends)])  325 us
    unnamed x4, waiting for transfers between devices  219 us
    ppermute x24, starting transfers between devices, partner_2(): return lax.ppermute(block, axis, route)  130 us
    unnamed x1, blocking collectives  108 us
    slice x68, local copies, waits for them, and re-layouts, forward_pass(): stored_inputs[copy_index]  105 us
    dynamic_update_slice x68, other arithmetic, forward_pass(): lax.dynamic_update_slice(stored_inputs, kept[None, None], corner)  104 us
    slice x68, local copies, waits for them, and re-layouts, forward_pass(): exit_cotangents[copy_index]  83.6 us
  transfers between devices with their start and end apart: 95, of which 52 were waited for; matrix products, arithmetic and copies ran while one was open for 2% of the time, Pallas kernels for 0%

commit v1 on v0

v1 whole, which is shorter than its diff:
```python
import functools
import math

import jax
import jax.numpy as jnp
from jax import lax
from jax.experimental import pallas as pl
from jax.experimental.pallas import tpu as pltpu
from jax.sharding import PartitionSpec as P

MESH = pl.DeviceIdType.MESH
HEAD = 64
QHEADS = 7
QDIM = HEAD * QHEADS
QKV = QDIM + 2 * HEAD
D = 896
ROWS = 32
CORES = 2
EPS = 1e-06
F32 = jnp.float32
BF16 = jnp.bfloat16
NT = (((1,), (1,)), ((), ()))
TN = (((0,), (0,)), ((), ()))


def dot(a, b, dims=None):
    if dims is None:
        return jnp.dot(a, b, preferred_element_type=F32)
    return lax.dot_general(a, b, dims, preferred_element_type=F32)


def low_half():
    return lax.broadcasted_iota(jnp.int32, (ROWS, 128), 1) < HEAD


def stack_heads(tiles):
    low = low_half()
    parts = []
    for head in range(QHEADS):
        tile = tiles[head // 2]
        parts.append(jnp.where(low if head % 2 == 0 else ~low, tile, 0.0))
    return jnp.concatenate(parts, axis=0).astype(BF16)


def unstack_heads(stacked, last):
    low = low_half()
    tiles = []
    for pair in range(QHEADS // 2):
        base = pair * 2 * ROWS
        tiles.append(jnp.where(low, stacked[base : base + ROWS], stacked[base + ROWS : base + 2 * ROWS]))
    tiles.append(jnp.where(low, stacked[6 * ROWS : 7 * ROWS], last))
    return tiles


def both_halves(tile, from_low):
    turned = pltpu.roll(tile, HEAD, 1)
    low = low_half()
    return jnp.where(low, tile, turned) if from_low else jnp.where(low, turned, tile)


def widen(tile):
    return jnp.concatenate([tile, jnp.zeros_like(tile)], axis=1)


def relay_kernel(
    geo,
    states_ref,
    wq_sh,
    wo_sh,
    fg_ref,
    vw_ref,
    pos_ref,
    want_ref,
    gq_out,
    go_out,
    dg_out,
    bq,
    bo,
    tq,
    to,
    wqf,
    wof,
    gp,
    gs,
    xs,
    ns,
    qst,
    kd,
    vd,
    ps,
    at,
    rr,
    cs,
    dps,
    gq,
    go,
    rq0,
    ro0,
    r1q,
    r1o,
    so,
    r2q,
    r2o,
    sq3,
    so3,
    r3q,
    r3o,
    fq,
    fo,
    dg,
    dgr,
    ss,
    rs,
):
    nst, ny, nx, nz = geo
    nc = CORES
    ndp = nx * nz * nc
    rq, ro = D // ndp, QDIM // ndp
    gqr, gor = D // nx, QDIM // nx
    p, d = lax.axis_index("pipe"), lax.axis_index("dp")
    div, rem = lax.div, lax.rem
    stage, y = div(p, ny), rem(p, ny)
    x, z, c = div(d, nz * nc), rem(div(d, nc), nz), rem(d, nc)
    slots = {}

    def slot(*name):
        return slots.setdefault(name, len(slots))

    def rcopy(src, dst, name, dev):
        i = slot(*name)
        return pltpu.make_async_remote_copy(
            src_ref=src,
            dst_ref=dst,
            send_sem=ss.at[i],
            recv_sem=rs.at[i],
            device_id=dev,
            device_id_type=MESH,
        )

    def dpi(xx, zz, cc):
        return (xx * nz + zz) * nc + cc

    partner = (p, dpi(x, z, 1 - c))
    zdev = [(p, dpi(x, rem(z + t, nz), c)) for t in range(nz)]
    xdev = [(p, dpi(rem(x + t, nx), z, c)) for t in range(nx)]
    ydev = [(stage * ny + rem(y + t, ny), d) for t in range(ny)]
    nextdev = (rem(stage + 1, nst) * ny + y, d)
    prevdev = (rem(stage + nst - 1, nst) * ny + y, d)
    zf = [rem(z + nz - t, nz) for t in range(nz)]
    zt = [rem(z + t, nz) for t in range(nz)]
    xf_ = [rem(x + nx - t, nx) for t in range(nx)]
    xt_ = [rem(x + t, nx) for t in range(nx)]
    yf_ = [rem(y + ny - t, ny) for t in range(ny)]
    yt_ = [rem(y + t, ny) for t in range(ny)]
    pending = []

    def V(ref, *place):
        return ref, place

    def view(spot):
        ref, place = spot
        return ref.at[place] if place else ref

    def send(src, dst, name, dev, group="all"):
        make = lambda: rcopy(view(src), view(dst), name, dev)
        make().start()
        pending.append((group, make))

    def recv(ref, name):
        rcopy(view(ref), view(ref), name, partner).wait_recv()

    def starts(places, size):
        return [pl.ds(pl.multiple_of(place * size, 16), size) for place in places]

    q_from, q_to = starts(xf_, gqr), starts(xt_, gqr)
    o_from, o_to = starts(xf_, gor), starts(xt_, gor)

    peers = [partner] + zdev[1:] + xdev[1:] + ydev[1:]
    if nst > 1:
        peers = peers + [nextdev, prevdev]
    barrier = pltpu.get_barrier_semaphore()
    for dev in peers:
        pl.semaphore_signal(barrier, inc=1, device_id=dev, device_id_type=MESH)
    pl.semaphore_wait(barrier, len(peers))

    i_me = z * nc + c
    for t in range(1, nz):
        send(V(wq_sh), V(bq, i_me), ("zq", t), zdev[t])
        send(V(wo_sh), V(bo, i_me), ("zo", t), zdev[t])
    send(V(wq_sh), V(bq, i_me), ("pq", 0), partner)
    send(V(wo_sh), V(bo, i_me), ("po", 0), partner)
    bq[i_me] = wq_sh[...]
    bo[i_me] = wo_sh[...]
    for t in range(1, nz):
        i_f = zf[t] * nc + c
        recv(V(bq, i_f), ("zq", t))
        send(V(bq, i_f), V(bq, i_f), ("pq", t), partner)
        recv(V(bo, i_f), ("zo", t))
        send(V(bo, i_f), V(bo, i_f), ("po", t), partner)
    for t in range(nz):
        i_f = zf[t] * nc + 1 - c
        recv(V(bq, i_f), ("pq", t))
        recv(V(bo, i_f), ("po", t))

    @pl.when(c == 0)
    def _():
        for i in range(nz * nc):
            tq[rq * i : rq * (i + 1), :] = bq[i].astype(F32)
        wqf[y, q_to[0], :] = tq[...].astype(BF16)
        mine = V(wqf, y, q_to[0])
        for t in range(1, nx):
            send(mine, mine, ("xq", t), xdev[t], "c0")
        for t in range(1, nx):
            recv(V(wqf, y, q_from[t]), ("xq", t))
        for t in range(1, ny):
            send(V(wqf, y), V(wqf, y), ("yq", t), ydev[t], "c0")
        send(V(wqf, y), V(wqf, y), ("fq", 0), partner, "c0")
        for t in range(1, ny):
            recv(V(wqf, yf_[t]), ("yq", t))
            send(V(wqf, yf_[t]), V(wqf, yf_[t]), ("fq", t), partner, "c0")
        for t in range(nx):
            recv(V(wof, pl.ds(0, ny), o_from[t]), ("fo", t))
            recv(V(gp, pl.ds(0, ny), xf_[t]), ("fg", t))

    @pl.when(c == 1)
    def _():
        gain = jnp.zeros((1, D), F32)
        for i in range(nz * nc):
            shard = bo[i].astype(F32)
            to[ro * i : ro * (i + 1), :] = shard[0:ro]
            gain = gain + shard[ro : ro + 1]
        wof[y, o_to[0], :] = to[...].astype(BF16)
        gp[y, x] = jnp.broadcast_to(gain, (8, D))
        mine = V(wof, y, o_to[0])
        for t in range(1, ny):
            send(mine, mine, ("yo", t), ydev[t], "c1")
            send(V(gp, y, x), V(gp, y, x), ("yg", t), ydev[t], "c1")
        for t in range(1, ny):
            recv(V(wof, yf_[t], o_to[0]), ("yo", t))
            recv(V(gp, yf_[t], x), ("yg", t))

        def block(t):
            return V(wof, pl.ds(0, ny), o_from[t])

        for t in range(1, nx):
            send(block(0), block(0), ("xo", t), xdev[t], "c1")
            send(V(gp, pl.ds(0, ny), x), V(gp, pl.ds(0, ny), x), ("xg", t), xdev[t], "c1")
        send(block(0), block(0), ("fo", 0), partner, "c1")
        send(V(gp, pl.ds(0, ny), x), V(gp, pl.ds(0, ny), x), ("fg", 0), partner, "c1")
        for t in range(1, nx):
            recv(block(t), ("xo", t))
            send(block(t), block(t), ("fo", t), partner, "c1")
            recv(V(gp, pl.ds(0, ny), xf_[t]), ("xg", t))
            send(V(gp, pl.ds(0, ny), xf_[t]), V(gp, pl.ds(0, ny), xf_[t]), ("fg", t), partner, "c1")
        for t in range(ny):
            recv(V(wqf, yf_[t]), ("fq", t))

    for k in range(ny):
        total = gp[k, 0]
        for xx in range(1, nx):
            total = total + gp[k, xx]
        gs[k] = total
    dg[...] = jnp.zeros_like(dg)

    @pl.when(stage == 0)
    def _():
        xs[0] = states_ref[y]

    if nst > 1:

        @pl.when(stage > 0)
        def _():
            recv(V(xs, 0), ("hop",))

    def forward(k, carry):
        wide = xs[k].astype(F32)
        r = lax.rsqrt(jnp.sum(wide * wide, axis=-1, keepdims=True) * (1.0 / D) + EPS)
        rr[k] = jnp.broadcast_to(r, (ROWS, 128))
        normed = (wide * r * gs[k, 0:1, :]).astype(BF16)
        ns[k] = normed
        projected = dot(normed, wqf[k]).astype(BF16).astype(F32)
        tiles = [projected[:, 128 * i : 128 * (i + 1)] for i in range(4)]
        queries = stack_heads(tiles)
        keys = both_halves(tiles[3], False).astype(BF16)
        values = both_halves(widen(projected[:, 4 * 128 :]), True).astype(BF16)
        qst[k], kd[k], vd[k] = queries, keys, values
        scores = dot(keys, queries, NT) * (1.0 / math.sqrt(HEAD))
        key_at = lax.broadcasted_iota(jnp.int32, scores.shape, 0)
        query_at = lax.broadcasted_iota(jnp.int32, scores.shape, 1) & (ROWS - 1)
        scores = jnp.where(query_at >= key_at, scores, -1e30)
        weights = jnp.exp(scores - jnp.max(scores, axis=0, keepdims=True))
        attention = weights / jnp.sum(weights, axis=0, keepdims=True)
        ps[k] = attention
        attended = unstack_heads(dot(attention.astype(BF16), values, TN), 0.0)
        attended = jnp.concatenate(attended[:3] + [attended[3][:, :HEAD]], axis=1).astype(BF16)
        at[k] = attended
        xs[k + 1] = (wide + dot(attended, wof[k])).astype(BF16)
        return carry

    lax.fori_loop(0, ny, forward, 0)

    if nst > 1:

        @pl.when(stage < nst - 1)
        def _():
            send(V(xs, ny), V(xs, 0), ("hop",), nextdev, "up")

    @pl.when(stage == nst - 1)
    def _():
        wide = xs[ny].astype(F32)
        w = fg_ref[...].astype(F32) * vw_ref[...].astype(F32)
        r = lax.rsqrt(jnp.sum(wide * wide, axis=-1, keepdims=True) * (1.0 / D) + EPS)
        predicted = r * jnp.sum(wide * w, axis=-1, keepdims=True)
        chosen = pos_ref[pl.ds(y, 1), :]
        wanted = want_ref[pl.ds(y, 1), :]
        at_row = lax.broadcasted_iota(jnp.int32, (ROWS, chosen.shape[1]), 0)
        selector = (at_row == chosen).astype(F32)
        residual = jnp.sum(selector * predicted, axis=0, keepdims=True) - wanted
        slope = jnp.sum(selector * residual, axis=1, keepdims=True)
        cs[ny] = (slope * (r * w - wide * (r * r * predicted * (1.0 / D)))).astype(BF16)

    if nst > 1:

        @pl.when(stage < nst - 1)
        def _():
            recv(V(cs, ny), ("back",))

    def backward(step, carry):
        k = ny - 1 - step
        cot = cs[k + 1]
        d_att = dot(cot, wof[k], NT)
        tiles = [d_att[:, 128 * i : 128 * (i + 1)] for i in range(3)] + [widen(d_att[:, 3 * 128 :])]
        stacked = stack_heads(tiles)
        attention = ps[k]
        d_attention = dot(vd[k], stacked, NT)
        inner = jnp.sum(d_attention * attention, axis=0, keepdims=True)
        d_scores = (attention * (d_attention - inner) * (1.0 / math.sqrt(HEAD))).astype(BF16)
        d_values = dot(attention.astype(BF16), stacked)
        d_keys = dot(d_scores, qst[k])
        d_queries = dot(d_scores, kd[k], TN)
        d_values = d_values + pltpu.roll(d_values, HEAD, 1)
        d_keys = d_keys + pltpu.roll(d_keys, HEAD, 1)
        d_proj = unstack_heads(d_queries, d_keys) + [d_values[:, :HEAD]]
        d_proj = jnp.concatenate(d_proj, axis=1).astype(BF16)
        dps[k] = d_proj
        d_normed = dot(d_proj, wqf[k], NT)
        wide = xs[k].astype(F32)
        r = rr[k][:, 0:1]
        unit = wide * r
        dg[pl.ds(k, 1), :] = jnp.sum(d_normed * unit, axis=0, keepdims=True)
        scaled = d_normed * gs[k, 0:1, :]
        mean = jnp.sum(scaled * unit, axis=-1, keepdims=True) * (1.0 / D)
        cs[k] = (cot.astype(F32) + r * (scaled - unit * mean)).astype(BF16)
        return carry

    lax.fori_loop(0, ny, backward, 0)

    if nst > 1:

        @pl.when(stage > 0)
        def _():
            send(V(cs, 0), V(cs, ny), ("back",), prevdev, "down")

    def weight_grads(k):
        gq[k] = dot(ns[k], dps[k], TN).astype(BF16)
        go[k] = dot(at[k], cs[k + 1], TN).astype(BF16)

    order = [t for t in range(1, ny)] + [0]

    def hand_over(t):
        k = yt_[t]

        @pl.when(c == 0)
        def _():
            send(V(go, k), V(ro0, k), ("r0", t), partner, "c0")

        @pl.when(c == 1)
        def _():
            send(V(gq, k), V(rq0, k), ("r0q", t), partner, "c1")

    def pass_on(t):
        k = yt_[t]

        @pl.when(c == 0)
        def _():
            recv(V(rq0, k), ("r0q", t))

            @pl.loop(0, D // 112)
            def _(i):
                rows = pl.ds(pl.multiple_of(i * 112, 16), 112)
                gq[k, rows, :] = (gq[k, rows, :].astype(F32) + rq0[k, rows, :].astype(F32)).astype(BF16)

            if t:
                send(V(gq, k), V(r1q, t - 1), ("r1q", t), ydev[t], "c0")

        @pl.when(c == 1)
        def _():
            recv(V(ro0, k), ("r0", t))

            @pl.loop(0, QDIM // 112)
            def _(i):
                rows = pl.ds(pl.multiple_of(i * 112, 16), 112)
                go[k, rows, :] = (go[k, rows, :].astype(F32) + ro0[k, rows, :].astype(F32)).astype(BF16)

            for u in range(1, nx):
                send(V(go, k, o_to[u]), V(r1o, u - 1, k), ("r1o", t, u), xdev[u], "c1")

    @pl.when(c == 0)
    def _():
        send(V(dg), V(dgr, 0), ("dg0",), partner, "c0")

    before = None
    for t in order:
        weight_grads(yt_[t])
        hand_over(t)
        if before is not None:
            pass_on(before)
        before = t
    pass_on(before)

    @pl.when(c == 0)
    def _():
        for t in range(1, ny):
            recv(V(r1q, t - 1), ("r1q", t))

        @pl.loop(0, D // 112)
        def _(i):
            rows = pl.ds(pl.multiple_of(i * 112, 16), 112)
            total = gq[y, rows, :].astype(F32)
            for t in range(1, ny):
                total = total + r1q[t - 1, rows, :].astype(F32)
            rq0[y, rows, :] = total.astype(BF16)

        for t in range(1, nx):
            send(V(rq0, y, q_to[t]), V(r2q, t - 1), ("r2q", t), xdev[t], "c0")
        for t in range(1, nx):
            recv(V(r2q, t - 1), ("r2q", t))
        total = rq0[y, q_to[0], :].astype(F32)
        for t in range(1, nx):
            total = total + r2q[t - 1].astype(F32)
        tq[...] = total
        for i in range(nz * nc):
            sq3[i // nc, i % nc] = tq[rq * i : rq * (i + 1), :].astype(BF16)
        for t in range(1, nz):
            send(V(sq3, zt[t]), V(r3q, t - 1), ("r3q", t), zdev[t], "c0")
        for t in range(1, nz):
            recv(V(r3q, t - 1), ("r3q", t))
        for cc in range(nc):
            total = sq3[z, cc].astype(F32)
            for t in range(1, nz):
                total = total + r3q[t - 1, cc].astype(F32)
            if cc == 0:
                gq_out[...] = total
            else:
                fq[0] = total
        send(V(fq, 0), V(fq, 1), ("f4q",), partner, "c0")
        recv(V(fo, 1), ("f4o",))
        go_out[...] = fo[1]
        recv(V(dgr, 1), ("dg4",))
        dg_out[...] = dgr[1]

    @pl.when(c == 1)
    def _():
        recv(V(dgr, 0), ("dg0",))
        gains = dg[...] + dgr[0]
        dgr[2] = gains
        for t in range(1, nx):
            send(V(dgr, 2), V(dgr, 5 + t), ("dgx", t), xdev[t], "c1")
        for k in range(ny):
            base = go[k, o_to[0], :].astype(F32)
            so[k] = base
        for u in range(ny):
            k = yt_[u]
            for t in range(1, nx):
                recv(V(r1o, t - 1, yt_[u]), ("r1o", u, t))
            total = so[k]
            for t in range(1, nx):
                total = total + r1o[t - 1, k].astype(F32)
            ro0[k, 0:gor, :] = total.astype(BF16)
            if u:
                send(V(ro0, k, pl.ds(0, gor)), V(r2o, u - 1), ("r2o", u), ydev[u], "c1")
        for t in range(1, nx):
            recv(V(dgr, 5 + t), ("dgx", t))
            gains = gains + dgr[5 + t]
        dgr[3] = gains
        for t in range(1, ny):
            send(V(dgr, 3), V(dgr, 8 + t), ("dgy", t), ydev[t], "c1")
        for t in range(1, ny):
            recv(V(r2o, t - 1), ("r2o", t))
        total = ro0[y, 0:gor, :].astype(F32)
        for t in range(1, ny):
            total = total + r2o[t - 1].astype(F32)
        to[...] = total
        for i in range(nz * nc):
            so3[i // nc, i % nc] = to[ro * i : ro * (i + 1), :].astype(BF16)
        for t in range(1, nz):
            send(V(so3, zt[t]), V(r3o, t - 1), ("r3o", t), zdev[t], "c1")
        for t in range(1, ny):
            recv(V(dgr, 8 + t), ("dgy", t))
            gains = gains + dgr[8 + t]
        dgr[4] = gains
        for t in range(1, nz):
            send(V(dgr, 4), V(dgr, 11 + t), ("dgz", t), zdev[t], "c1")
        for t in range(1, nz):
            recv(V(r3o, t - 1), ("r3o", t))
        for cc in range(nc):
            total = so3[z, cc].astype(F32)
            for t in range(1, nz):
                total = total + r3o[t - 1, cc].astype(F32)
            if cc == 1:
                go_out[...] = total
            else:
                fo[0] = total
        send(V(fo, 0), V(fo, 1), ("f4o",), partner, "c1")
        for t in range(1, nz):
            recv(V(dgr, 11 + t), ("dgz", t))
            gains = gains + dgr[11 + t]
        dgr[5] = gains
        send(V(dgr, 5), V(dgr, 1), ("dg4",), partner, "c1")
        dg_out[...] = gains
        recv(V(fq, 1), ("f4q",))
        gq_out[...] = fq[1]

    conditions = {"all": None, "c0": c == 0, "c1": c == 1, "up": stage < nst - 1, "down": stage > 0}
    for group, condition in conditions.items():
        makers = [make for name, make in pending if name == group]
        if not makers:
            continue
        if condition is None:
            for make in makers:
                make().wait_send()
        else:

            @pl.when(condition)
            def _():
                for make in makers:
                    make().wait_send()


def scratch(geo):
    nst, ny, nx, nz = geo
    nc = CORES
    ndp = nx * nz * nc
    rq, ro = D // ndp, QDIM // ndp
    rop = -(-(ro + 1) // 16) * 16
    gqr, gor = D // nx, QDIM // nx
    v = pltpu.VMEM
    return [
        v((nz * nc, rq, QKV), BF16),
        v((nz * nc, rop, D), BF16),
        v((gqr, QKV), F32),
        v((gor, D), F32),
        v((ny, D, QKV), BF16),
        v((ny, QDIM, D), BF16),
        v((ny, nx, 8, D), F32),
        v((ny, 8, D), F32),
        v((ny + 1, ROWS, D), BF16),
        v((ny, ROWS, D), BF16),
        v((ny, QHEADS * ROWS, 128), BF16),
        v((ny, ROWS, 128), BF16),
        v((ny, ROWS, 128), BF16),
        v((ny, ROWS, QHEADS * ROWS), F32),
        v((ny, ROWS, QDIM), BF16),
        v((ny, ROWS, 128), F32),
        v((ny + 1, ROWS, D), BF16),
        v((ny, ROWS, QKV), BF16),
        v((ny, D, QKV), BF16),
        v((ny, QDIM, D), BF16),
        v((ny, D, QKV), BF16),
        v((ny, QDIM, D), BF16),
        v((max(ny - 1, 1), D, QKV), BF16),
        v((max(nx - 1, 1), ny, gor, D), BF16),
        v((ny, gor, D), F32),
        v((max(nx - 1, 1), gqr, QKV), BF16),
        v((max(ny - 1, 1), gor, D), BF16),
        v((nz, nc, rq, QKV), BF16),
        v((nz, nc, ro, D), BF16),
        v((max(nz - 1, 1), nc, rq, QKV), BF16),
        v((max(nz - 1, 1), nc, ro, D), BF16),
        v((2, rq, QKV), F32),
        v((2, ro, D), F32),
        v((8, D), F32),
        v((15, 8, D), F32),
        pltpu.SemaphoreType.DMA((96,)),
        pltpu.SemaphoreType.DMA((96,)),
    ]


def per_device(geo, states, norm_gain, qkv_weight, out_weight, final_gain, value_weight, positions, targets):
    nst, ny, nx, nz = geo
    ndp = nx * nz * CORES
    rq, ro = D // ndp, QDIM // ndp
    rop = -(-(ro + 1) // 16) * 16
    d = lax.axis_index("dp")
    y = lax.axis_index("pipe") % ny
    lanes = lax.broadcasted_iota(jnp.int32, (ndp, rq), 0)
    gain_row = jnp.where(lanes == d, norm_gain, 0).reshape(1, D)
    wo = jnp.concatenate([out_weight[0], gain_row, jnp.zeros((rop - ro - 1, D), BF16)], axis=0)
    windows = states.shape[0] * states.shape[1]
    vmem = pl.BlockSpec(memory_space=pltpu.VMEM)
    gq, go, dg = pl.pallas_call(
        functools.partial(relay_kernel, geo),
        out_shape=(
            jax.ShapeDtypeStruct((rq, QKV), F32),
            jax.ShapeDtypeStruct((ro, D), F32),
            jax.ShapeDtypeStruct((8, D), F32),
        ),
        in_specs=[vmem] * 7,
        out_specs=(vmem, vmem, vmem),
        scratch_shapes=scratch(geo),
        compiler_params=pltpu.CompilerParams(
            collective_id=0, has_side_effects=True, vmem_limit_bytes=56 * 1024 * 1024
        ),
        name="relay",
    )(
        states.reshape(windows, ROWS, D),
        qkv_weight[0],
        wo,
        final_gain.reshape(1, D),
        value_weight.reshape(1, D),
        positions.reshape(windows, -1),
        targets.reshape(windows, -1),
    )
    grad_gain = lax.dynamic_slice(dg, (y, d * rq), (1, rq))
    return grad_gain, gq[None], go[None]


def solution(mesh, geo=(4, 4, 4, 4)):
    return jax.shard_map(
        functools.partial(per_device, geo),
        mesh=mesh,
        in_specs=(
            P(None, None, "dp", None),
            P("pipe", "dp"),
            P("pipe", "dp", None),
            P("pipe", "dp", None),
            P(),
            P(),
            P(None, None, "dp", None),
            P(None, None, "dp", None),
        ),
        out_specs=(P("pipe", "dp"), P("pipe", "dp", None), P("pipe", "dp", None)),
        check_vma=False,
    )
```

time: 2150 us -> 192 us (0.09)
  starting transfers between devices: 645 us -> 0 us
  waiting for transfers between devices: 598 us -> 0 us
  local copies, waits for them, and re-layouts: 399 us -> 5.68 us
  other arithmetic: 217 us -> 0.77 us
  Pallas kernels: 0 us -> 184 us
  blocking collectives: 162 us -> 0 us
  matrix products: 88 us -> 0 us
    ppermute x92 -> x0, starting transfers between devices: 644 us -> none  [the longest x34 471 us: extended(): lax.ppermute(tail, axis, [(i, (i + 1) % count) for i in range(ends)])]
    ppermute x92 -> x0, waiting for transfers between devices: 366 us -> none  [the longest x34 325 us: extended(): lax.ppermute(head, axis, [((i + 1) % count, i) for i in range(ends)])]
    slice x192 -> x0, local copies, waits for them, and re-layouts: 256 us -> none  [the longest x68 105 us: forward_pass(): stored_inputs[copy_index]]
    unnamed x4 -> x0, waiting for transfers between devices: 219 us -> none
    pallas_call x0 -> x1, Pallas kernels: none -> 184 us  [per_device(): pl.pallas_call(functools.partial(relay_kernel, geo), out_shape=(jax.Shape...]
    dynamic_update_slice x102 -> x0, other arithmetic: 126 us -> none  [the longest x68 104 us: forward_pass(): lax.dynamic_update_slice(stored_inputs, kept[None, None], corner)]
    unnamed x1 -> x0, blocking collectives: 108 us -> none
    dot_general x60 -> x0, matrix products: 86.9 us -> none  [the longest x16 31.7 us: section_apply(): jnp.dot(normed, qkv_mat, preferred_element_type=jnp.float32)]
  transfers between devices with their start and end apart: 95 -> 0, of which waited for: 52 -> 0; matrix products, arithmetic and copies ran while one was open for 2% -> 0% of each run, Pallas kernels for 0% -> 0%
where the time goes in v1:
time: 192 us
  Pallas kernels  184 us (96%)
  local copies, waits for them, and re-layouts  5.68 us (3%)
    pallas_call x1, Pallas kernels, per_device(): pl.pallas_call(functools.partial(relay_kernel, geo), out_shape=(jax.Shape...  184 us

profile of v1, /device:TPU:1, one launch (start us, length us, event | category | flops | bytes accessed | tf_op | source)
XLA Modules:
  0.0 191.6 jit_solution(15882148433682878740)
XLA Ops:
  0.6 0.0 copy-start.2
  0.7 0.0 copy-start.1
  0.7 0.1 pad.2.clone
  0.8 0.6 copy-done.2
  1.3 0.0 copy-start.3
  1.3 0.6 reshape.46.fg_ref
  1.9 0.1 copy-done.3
  2.0 0.0 copy-start.4
  2.0 0.6 reshape.47.vw_ref
  2.6 0.1 copy-done.4
  2.7 0.1 broadcast_select_fusion
  2.8 0.1 select_n.28
  2.9 0.0 copy-done.1
  2.9 0.7 maximum_maximum_fusion.wo_sh
  3.6 184.4 %relay.1 = (f32[28,576]{1,0:T(8,128)}, f32[14,896]{1,0:T(8,128)}, f32[8,896]{1,0:T(8,128)}) custom-call(bf16[4,32,896]{2,1,0:T(8,128)(2,1)} %bitcast.9, bf16[28,576]{1,0:T(8,128)(2,1)} %bitcast.12, bf16[16,896]{1,0:T(8,128)(2,1)} %maximum_maximum_fusion.wo_sh, bf16[1,896]{1,0:T(2,128)(2,1)} %reshape.46.fg_ref, bf16[1,896]{1,0:T(2,128)(2,1)} %reshape.47.vw_ref, ...), custom_call_target="tpu_custom_call" | custom-call | tf_op jit(solution)/shard_map/relay/pallas_call | solution.py:601
  188.0 1.3 dynamic_slice.3
  189.3 0.0 copy-start
  189.3 1.6 copy.11
  190.9 0.0 copy-done
  190.9 0.7 copy.12
  (1 shorter events, 0.0 us)
Async XLA Ops:
  0.6 0.7 copy-start.2
  0.7 2.2 %copy-start.1 = (bf16[1,14,896]{2,1,0:T(8,128)(2,1)S(1)}, bf16[1,14,896]{2,1,0:T(8,128)(2,1)}, u32[]{:S(2)}) copy-start(bf16[1,14,896]{2,1,0:T(8,128)(2,1)} %param.11) | copy-start | bytes 75268
  1.3 0.7 copy-start.3
  2.0 0.7 copy-start.4
  189.3 1.6 copy-start
